TPU v7x, 256 devices: a whole 4x4x8 slice. The times are simulated.
256 devices in a mesh: expert: 64 (over z, x, core), tensor: 4 (over y).
Axes of the slice: x: 4, y: 4, z: 8, core: 2. Of those that a mesh axis runs over, the one named last changes fastest.
Arguments:
- tokens: bfloat16 [2048, 4096], P('expert', 'tensor'), may hold values from -6 to 6
- cotangent: bfloat16 [2048, 4096], P('expert', 'tensor'), may hold values from -6 to 6
- routing: int32 [2048, 8], P('expert'), may hold values from 0 to 63, as said below
- gates: float32 [2048, 8], P('expert'), may hold values from 0.1 to 0.4
- w_in: bfloat16 [64, 4096, 1536], P('expert', None, 'tensor'), may hold values from -0.09375 to 0.09375
- w_out: bfloat16 [64, 1536, 4096], P('expert', 'tensor'), may hold values from -0.15625 to 0.15625
Outputs:
- mixed: bfloat16 [2048, 4096], P('expert', 'tensor')
- d_tokens: bfloat16 [2048, 4096], P('expert', 'tensor')
- d_w_in: bfloat16 [64, 4096, 1536], P('expert', None, 'tensor')
- d_w_out: bfloat16 [64, 1536, 4096], P('expert', 'tensor')
Inputs may be any that keep to these rules, and one draw needn't show every extreme that they name: `routing`: each row names 8 different experts. In each aligned block of 32 rows (the tokens of one index of the expert axis) no expert is named by more than 8 rows, and one expert is named by exactly 8 rows of every block.
All inputs are finite; a program needn't handle non-finite values.
Results may differ from a plain program's by a relative error of at most 0.0058.
Values may be sent and summed in bfloat16 or wider, within the bound.
A program may use at most 128 MiB of HBM per device.

v0:
```python
import jax
import jax.numpy as jnp
from jax import lax
from jax.sharding import PartitionSpec as P


def shards(tokens, cotangent, routing, gates, w_in, w_out):
    devices = lax.axis_size("expert")
    local_experts = w_in.shape[0]
    experts = devices * local_experts
    tok_rows = routing.shape[0]
    capacity = tok_rows // 4
    buffer_rows = experts * capacity
    highest = lax.Precision.HIGHEST
    matches = (routing[:, :, None] == jnp.arange(experts, dtype=jnp.int32)[None, None, :]).astype(
        jnp.int32
    )
    per_token = jnp.sum(matches, axis=1)
    earlier = jnp.cumsum(per_token, axis=0) - per_token
    destination = routing * capacity + jnp.take_along_axis(earlier, routing, axis=1)
    placed = (
        destination[:, :, None] == jnp.arange(buffer_rows, dtype=jnp.int32)[None, None, :]
    ).astype(jnp.float32)
    membership = jnp.sum(placed, axis=1)
    weighting = jnp.sum(placed * gates[:, :, None], axis=1)
    quarter = tokens.shape[1]
    rows = jnp.einsum(
        "tr,td->rd", membership.astype(jnp.bfloat16), tokens, preferred_element_type=jnp.float32
    ).astype(jnp.bfloat16)
    scaled = jnp.einsum(
        "tr,td->rd", weighting, cotangent.astype(jnp.float32), precision=highest
    ).astype(jnp.bfloat16)
    send = jnp.concatenate(
        [
            rows.reshape(devices, local_experts, capacity, quarter),
            scaled.reshape(devices, local_experts, capacity, quarter),
        ],
        axis=2,
    )
    arrived = lax.all_to_all(send, "expert", split_axis=0, concat_axis=0, tiled=True)
    whole = lax.all_gather(arrived, "tensor", axis=3, tiled=True)
    expert_rows = whole[:, :, :capacity]
    expert_scaled = whole[:, :, capacity:]
    preact = jnp.einsum("nesd,edh->nesh", expert_rows, w_in, preferred_element_type=jnp.float32)
    sigmoid_val = jax.nn.sigmoid(preact)
    hidden = (preact * sigmoid_val).astype(jnp.bfloat16)
    out_part = jnp.einsum("nesh,ehd->nesd", hidden, w_out, preferred_element_type=jnp.float32)
    grad_hidden = jnp.einsum(
        "nesd,ehd->nesh", expert_scaled, w_out, preferred_element_type=jnp.float32
    )
    grad_preact = (grad_hidden * sigmoid_val * (1.0 + preact * (1.0 - sigmoid_val))).astype(
        jnp.bfloat16
    )
    d_w_out = jnp.einsum(
        "nesh,nesd->ehd", hidden, expert_scaled, preferred_element_type=jnp.float32
    ).astype(jnp.bfloat16)
    d_w_in = jnp.einsum(
        "nesd,nesh->edh", expert_rows, grad_preact, preferred_element_type=jnp.float32
    ).astype(jnp.bfloat16)
    grad_part = jnp.einsum("nesh,edh->nesd", grad_preact, w_in, preferred_element_type=jnp.float32)
    parts = jnp.concatenate([out_part.astype(jnp.bfloat16), grad_part.astype(jnp.bfloat16)], axis=2)
    sums = lax.psum_scatter(parts, "tensor", scatter_dimension=3, tiled=True)
    back = lax.all_to_all(sums, "expert", split_axis=0, concat_axis=0, tiled=True)
    back_out = back[:, :, :capacity].reshape(buffer_rows, quarter).astype(jnp.float32)
    back_grad = back[:, :, capacity:].reshape(buffer_rows, quarter).astype(jnp.float32)
    mixed = jnp.einsum("tr,rd->td", weighting, back_out, precision=highest).astype(jnp.bfloat16)
    d_tokens = jnp.einsum("tr,rd->td", membership, back_grad, precision=highest).astype(
        jnp.bfloat16
    )
    return (mixed, d_tokens, d_w_in, d_w_out)


def solution(mesh):
    placed = (
        P("expert", "tensor"),
        P("expert", "tensor"),
        P("expert", None),
        P("expert", None),
        P("expert", None, "tensor"),
        P("expert", "tensor", None),
    )
    return jax.shard_map(
        shards,
        mesh=mesh,
        in_specs=placed,
        out_specs=(
            P("expert", "tensor"),
            P("expert", "tensor"),
            P("expert", None, "tensor"),
            P("expert", "tensor", None),
        ),
        check_vma=False,
    )
```

profile of v0, /device:TPU:2, one launch (start us, length us, event | category | flops | bytes accessed | tf_op | source)
XLA Modules:
  0.0 343.1 jit_solution(5815221899172722763)
XLA Ops:
  7.2 0.8 bitcast_or_fusion
  8.1 0.8 copy.47
  8.9 0.1 copy.48
  9.0 0.1 reshape.77
  9.1 0.8 copy.51
  9.8 0.1 convert_reduce_fusion.1
  9.9 0.1 reduce_window_sum.11
  10.0 1.9 gather_fusion
  12.0 0.1 reshape.80
  12.1 0.1 copy.49
  12.2 0.1 copy.50
  12.2 0.4 convert_reduce_fusion
  12.6 0.5 fusion.10
  13.1 1.0 fusion.11
  14.1 0.2 pad_maximum_fusion.1
  14.4 63.2 %all_to_all.10 = bf16[64,1,16,1024]{3,2,1,0:T(8,128)(2,1)} all-to-all(bf16[64,1,16,1024]{3,2,1,0:T(8,128)(2,1)S(1)} %pad_maximum_fusion.1), channel_id=1, replica_groups=mesh['expert'=64,'tensor'=4] {'expert'}, dimensions={0} | all-to-all | bytes 4194304 | tf_op jit(solution)/shard_map/all_to_all | solution.py:40
  77.6 0.2 reduce-scatter.2.cloned.1.call-start
  77.8 82.0 %all-gather.2.cloned.1.call-done = bf16[64,1,16,4096]{3,2,0,1:T(8,128)(2,1)} async-done(((bf16[64,1,16,1024]{3,2,0,1:T(8,128)(2,1)}), bf16[64,1,16,4096]{3,2,0,1:T(8,128)(2,1)}) %all-gather.2.cloned.1.call-update) | async-done | bytes 8388624 | tf_op jit(solution)/shard_map/all_gather | solution.py:41
  159.8 5.5 %fusion.18 = f32[64,1,8,384]{3,2,0,1:T(8,128)S(1)} fusion(bf16[1,4096,384]{2,1,0:T(8,128)(2,1)} %param.10, bf16[64,1,16,4096]{3,2,0,1:T(8,128)(2,1)} %all-gather.2.cloned.1.call-done), kind=kOutput, calls=%fused_computation.25 | convolution fusion | flops 1610612736 | bytes 8126464 | tf_op jit(solution)/shard_map/nesd,edh->nesh/dot_general | solution.py:44
  165.3 4.3 %fusion = bf16[64,1,8,4096]{3,2,0,1:T(8,128)(2,1)} fusion(bf16[1,384,4096]{2,1,0:T(8,128)(2,1)S(1)} %copy-done, f32[64,1,8,384]{3,2,0,1:T(8,128)S(1)} %fusion.18), kind=kOutput, calls=%fused_computation.6 | convolution fusion | flops 1613692928 | bytes 8126464 | tf_op jit(solution)/shard_map/nesh,ehd->nesd/dot_general | solution.py:47
  169.6 0.1 copy-done.4
  169.8 2.4 fusion.27
  172.2 0.8 copy-done.6
  173.0 4.3 %fusion.1 = bf16[64,1,8,4096]{3,2,0,1:T(8,128)(2,1)} fusion(bf16[64,8,384]{2,1,0:T(8,128)(2,1)S(1)} %fusion.27, bf16[1,4096,384]{2,1,0:T(8,128)(2,1)S(1)} %copy-done.5), kind=kOutput, calls=%fused_computation.7 | convolution fusion | flops 1612709888 | bytes 7733248 | tf_op jit(solution)/shard_map/nesh,edh->nesd/dot_general | solution.py:60
  177.4 7.8 %pad_maximum_fusion = bf16[64,1,16,4096]{3,2,0,1:T(8,128)(2,1)} fusion(bf16[64,1,8,4096]{3,2,0,1:T(8,128)(2,1)} %fusion.1, bf16[64,1,8,4096]{3,2,0,1:T(8,128)(2,1)} %fusion), kind=kLoop, calls=%fused_computation.1 | loop fusion | flops 16777216 | bytes 16777216 | tf_op jit(solution)/shard_map/concatenate | solution.py:61
  185.2 6.0 %fusion.3 = bf16[1,384,4096]{2,1,0:T(8,128)(2,1)} fusion(bf16[64,1,16,4096]{3,2,0,1:T(8,128)(2,1)} %all-gather.2.cloned.1.call-done, f32[64,1,8,384]{3,2,0,1:T(8,128)} %copy-done.7), kind=kOutput, calls=%fused_computation.9 | convolution fusion | flops 1613168640 | bytes 8126464 | tf_op jit(solution)/shard_map/nesh,nesd->ehd/dot_general | solution.py:54
  191.2 78.3 %reduce-scatter.2.cloned.1.call-done = bf16[64,1,16,1024]{3,2,0,1:T(8,128)(2,1)} async-done(((bf16[64,1,16,4096]{3,2,0,1:T(8,128)(2,1)}), bf16[64,1,16,1024]{3,2,0,1:T(8,128)(2,1)}) %reduce-scatter.2.cloned.1.call-update) | async-done | bytes 2097168 | tf_op jit(solution)/shard_map/reduce_scatter | solution.py:62
  269.4 10.7 %all-to-all-start.1 = ((bf16[64,1,16,1024]{3,2,1,0:T(8,128)(2,1)}), bf16[64,1,16,1024]{3,2,1,0:T(8,128)(2,1)}, u32[]{:S(2)}, u32[]{:S(2)}) async-start(bf16[64,1,16,1024]{3,2,1,0:T(8,128)(2,1)} %bitcast.123), calls=%async_computation.2 | async-start | bytes 4194304 | tf_op jit(solution)/shard_map/all_to_all | solution.py:63
  280.2 6.3 %fusion.2 = bf16[1,4096,384]{2,1,0:T(8,128)(2,1)} fusion(bf16[64,8,384]{2,1,0:T(8,128)(2,1)} %copy-done.6, bf16[64,1,16,4096]{3,2,0,1:T(8,128)(2,1)} %all-gather.2.cloned.1.call-done), kind=kOutput, calls=%fused_computation.8 | convolution fusion | flops 1612185600 | bytes 7733248 | tf_op jit(solution)/shard_map/nesd,nesh->edh/dot_general | solution.py:57
  286.5 44.9 %all-to-all-done.1 = bf16[64,1,16,1024]{3,2,1,0:T(8,128)(2,1)} async-done(((bf16[64,1,16,1024]{3,2,1,0:T(8,128)(2,1)}), bf16[64,1,16,1024]{3,2,1,0:T(8,128)(2,1)}, u32[]{:S(2)}, u32[]{:S(2)}) %all-to-all-start.1) | async-done | bytes 2097184 | tf_op jit(solution)/shard_map/all_to_all | solution.py:63
  331.3 2.5 convolution_convert_fusion.4
  333.8 2.5 convolution_convert_fusion.5
  (19 shorter events, 0.1 us)
Async XLA Ops:
  7.2 158.1 %copy-start = (bf16[1,384,4096]{2,1,0:T(8,128)(2,1)S(1)}, bf16[1,384,4096]{2,1,0:T(8,128)(2,1)}, u32[]{:S(2)}) copy-start(bf16[1,384,4096]{2,1,0:T(8,128)(2,1)} %param.11) | copy-start | bytes 9437188
  7.2 152.6 %all-gather.2.cloned.1.call-start = ((), (), s32[]{:S(2)}) async-start(), calls=%async_computation.3 | async-start | bytes 10485760 | tf_op jit(solution)/shard_map/all_gather | solution.py:41
  10.0 2.1 copy-start.3
  10.0 2.6 copy-start.1
  10.0 3.1 copy-start.2
  77.6 191.8 %reduce-scatter.2.cloned.1.call-start = ((), (), s32[]{:S(2)}) async-start(), calls=%async_computation.4 | async-start | bytes 10485760 | tf_op jit(solution)/shard_map/reduce_scatter | solution.py:62
  165.3 4.3 %copy-start.7 = (f32[64,1,8,384]{3,2,0,1:T(8,128)}, f32[64,1,8,384]{3,2,0,1:T(8,128)S(1)}, u32[]{:S(2)}) copy-start(f32[64,1,8,384]{3,2,0,1:T(8,128)S(1)} %fusion.18) | copy-start | bytes 2359300
  165.3 4.4 %copy-start.4 = (bf16[64,1,16,4096]{3,2,0,1:T(8,128)(2,1)S(1)}, bf16[64,1,16,4096]{3,2,0,1:T(8,128)(2,1)}, u32[]{:S(2)}) copy-start(bf16[64,1,16,4096]{3,2,0,1:T(8,128)(2,1)} %all-gather.2.cloned.1.call-done) | copy-start | bytes 25165828
  169.7 3.3 copy-start.5
  172.2 0.8 copy-start.6
  269.4 61.9 %all-to-all-start.1 = ((bf16[64,1,16,1024]{3,2,1,0:T(8,128)(2,1)}), bf16[64,1,16,1024]{3,2,1,0:T(8,128)(2,1)}, u32[]{:S(2)}, u32[]{:S(2)}) async-start(bf16[64,1,16,1024]{3,2,1,0:T(8,128)(2,1)} %bitcast.123), calls=%async_computation.2 | async-start | bytes 4194304 | tf_op jit(solution)/shard_map/all_to_all | solution.py:63
Sparse Core Ops, SparseCore 0:
  77.7 82.0 all-gather.1
  185.3 84.0 reduce-scatter.1
where the time goes:
time: 343 us
  waiting for transfers between devices  205 us (60%)
  blocking collectives  63.2 us (18%)
  matrix products  35.2 us (10%)
  between operations  14.2 us (4%)
  starting transfers between devices  11 us (3%)
  other arithmetic  9.46 us (3%)
  local copies, waits for them, and re-layouts  4.91 us (1%)
    all_gather x1, waiting for transfers between devices, shards(): whole = lax.all_gather(arrived, 'tensor', axis=3, tiled=True)  82 us
    reduce_scatter x1, waiting for transfers between devices, shards(): sums = lax.psum_scatter(parts, 'tensor', scatter_dimension=3, tiled=True)  78.3 us
    all_to_all x1, blocking collectives, shards(): lax.all_to_all(send, 'expert', split_axis=0, concat_axis=0, tiled=True)  63.2 us
    all_to_all x1, waiting for transfers between devices, shards(): lax.all_to_all(sums, 'expert', split_axis=0, concat_axis=0, tiled=True)  44.9 us
    all_to_all x1, starting transfers between devices, shards(): lax.all_to_all(sums, 'expert', split_axis=0, concat_axis=0, tiled=True)  10.7 us
    concatenate x1, other arithmetic, shards(): jnp.concatenate([out_part.astype(jnp.bfloat16), grad_part.astype(jnp.bflo...  7.8 us
  transfers between devices with their start and end apart: 3, of which 3 were waited for; matrix products, arithmetic and copies ran while one was open for 4% of the time, Pallas kernels for 0%

commit v1 on v0

--- a/solution.py
+++ b/solution.py
@@ -38,7 +38,28 @@
         axis=2,
     )
     arrived = lax.all_to_all(send, "expert", split_axis=0, concat_axis=0, tiled=True)
-    whole = lax.all_gather(arrived, "tensor", axis=3, tiled=True)
+    devices_2, position, width = (
+        lax.axis_size("tensor"),
+        lax.axis_index("tensor"),
+        arrived.shape[3],
+    )
+    upward = [(i, (i + 1) % devices_2) for i in range(devices_2)]
+    behind = [(i, (i - 1) % devices_2) for i in range(devices_2)]
+    out = jnp.zeros((*arrived.shape[:3], devices_2 * width, *arrived.shape[3 + 1 :]), arrived.dtype)
+    out = lax.dynamic_update_slice_in_dim(out, arrived, position * width, axis=3)
+    from_left = from_right = arrived
+    middle = devices_2 // 2
+    for turn in range(1, middle + 1):
+        from_left = lax.ppermute(from_left, "tensor", upward)
+        out = lax.dynamic_update_slice_in_dim(
+            out, from_left, (position - turn) % devices_2 * width, axis=3
+        )
+        if turn < devices_2 - middle:
+            from_right = lax.ppermute(from_right, "tensor", behind)
+            out = lax.dynamic_update_slice_in_dim(
+                out, from_right, (position + turn) % devices_2 * width, axis=3
+            )
+    whole = out
     expert_rows = whole[:, :, :capacity]
     expert_scaled = whole[:, :, capacity:]
     preact = jnp.einsum("nesd,edh->nesh", expert_rows, w_in, preferred_element_type=jnp.float32)

time: 343 us -> 350 us (1.020)
  local copies, waits for them, and re-layouts: 4.91 us -> 12.9 us
    ppermute x0 -> x3, waiting for transfers between devices: none -> 83.8 us  [the longest x2 83.8 us: shards(): from_left = lax.ppermute(from_left, 'tensor', upward)]
    all_gather x1 -> x0, waiting for transfers between devices: 82 us -> none  [shards(): whole = lax.all_gather(arrived, 'tensor', axis=3, tiled=True)]
    dynamic_update_slice x0 -> x4, local copies, waits for them, and re-layouts: none -> 7.64 us  [the longest x2 3.74 us: shards(): lax.dynamic_update_slice_in_dim(out, from_left, (position - turn) % devic...]
    reduce_scatter x1, waiting for transfers between devices: 78.3 us -> 74.2 us  [shards(): sums = lax.psum_scatter(parts, 'tensor', scatter_dimension=3, tiled=True)]
    ppermute x0 -> x3, starting transfers between devices: none -> 3.54 us  [the longest x2 1.88 us: shards(): from_left = lax.ppermute(from_left, 'tensor', upward)]
  transfers between devices with their start and end apart: 3 -> 5, of which waited for: 3 -> 4; matrix products, arithmetic and copies ran while one was open for 4% -> 6% of each run, Pallas kernels for 0% -> 0%
where the time goes in v1:
time: 350 us; the launch traced here: 349 us
  waiting for transfers between devices  203 us (58%)
  blocking collectives  63.2 us (18%)
  matrix products  32.3 us (9%)
  starting transfers between devices  14.3 us (4%)
  between operations  14.2 us (4%)
  local copies, waits for them, and re-layouts  12.9 us (4%)
  other arithmetic  9.3 us (3%)
    ppermute x2, waiting for transfers between devices, shards(): from_left = lax.ppermute(from_left, 'tensor', upward)  83.8 us
    reduce_scatter x1, waiting for transfers between devices, shards(): sums = lax.psum_scatter(parts, 'tensor', scatter_dimension=3, tiled=True)  74.2 us
    all_to_all x1, blocking collectives, shards(): lax.all_to_all(send, 'expert', split_axis=0, concat_axis=0, tiled=True)  63.2 us
    all_to_all x1, waiting for transfers between devices, shards(): lax.all_to_all(sums, 'expert', split_axis=0, concat_axis=0, tiled=True)  44.9 us
    all_to_all x1, starting transfers between devices, shards(): lax.all_to_all(sums, 'expert', split_axis=0, concat_axis=0, tiled=True)  10.8 us
    concatenate x1, other arithmetic, shards(): jnp.concatenate([out_part.astype(jnp.bfloat16), grad_part.astype(jnp.bflo...  7.8 us
  transfers between devices with their start and end apart: 5, of which 4 were waited for; matrix products, arithmetic and copies ran while one was open for 6% of the time, Pallas kernels for 0%

profile of v1, /device:TPU:2, one launch (start us, length us, event | category | flops | bytes accessed | tf_op | source)
XLA Modules:
  0.0 349.2 jit_solution(11719131081706814175)
XLA Ops:
  7.2 0.9 copy.51
  8.1 0.7 bitcast_or_fusion
  8.8 0.1 convert_reduce_fusion.1
  9.2 1.9 gather_fusion
  11.5 0.4 convert_reduce_fusion
  11.9 0.4 fusion.10
  12.4 1.0 fusion.11
  13.4 0.2 pad_maximum_fusion.1
  13.7 63.2 %all_to_all.10 = bf16[64,1,16,1024]{3,2,1,0:T(8,128)(2,1)} all-to-all(bf16[64,1,16,1024]{3,2,1,0:T(8,128)(2,1)S(1)} %pad_maximum_fusion.1), channel_id=1, replica_groups=mesh['expert'=64,'tensor'=4] {'expert'}, dimensions={0} | all-to-all | bytes 4194304 | tf_op jit(solution)/shard_map/all_to_all | solution.py:40
  76.8 1.6 collective-permute-start
  78.4 1.7 collective-permute-start.1
  80.1 44.3 %collective-permute-done = bf16[64,1,16,1024]{3,2,0,1:T(8,128)(2,1)} collective-permute-done((bf16[64,1,16,1024]{3,2,0,1:T(8,128)(2,1)}, bf16[64,1,16,1024]{3,2,0,1:T(8,128)(2,1)}, u32[]{:S(2)}, u32[]{:S(2)}) %collective-permute-start) | collective-permute-done | bytes 2097184 | tf_op jit(solution)/shard_map/ppermute | solution.py:53
  124.4 0.3 collective-permute-start.2
  124.7 1.0 broadcast_in_dim.7
  125.7 1.9 constant_dynamic-update-slice_fusion.3
  127.6 1.9 constant_dynamic-update-slice_fusion.2
  129.5 2.0 constant_dynamic-update-slice_fusion.1
  131.6 39.5 %collective-permute-done.2 = bf16[64,1,16,1024]{3,2,0,1:T(8,128)(2,1)} collective-permute-done((bf16[64,1,16,1024]{3,2,0,1:T(8,128)(2,1)}, bf16[64,1,16,1024]{3,2,0,1:T(8,128)(2,1)}, u32[]{:S(2)}, u32[]{:S(2)}) %collective-permute-start.2) | collective-permute-done | bytes 2097184 | tf_op jit(solution)/shard_map/ppermute | solution.py:53
  171.0 1.9 constant_dynamic-update-slice_fusion
  172.9 2.3 fusion.18
  175.3 0.9 copy-done.1
  176.1 2.4 fusion.27
  178.6 4.3 %fusion = bf16[64,1,8,4096]{3,2,0,1:T(8,128)(2,1)} fusion(bf16[1,384,4096]{2,1,0:T(8,128)(2,1)S(1)} %copy-done, f32[64,1,8,384]{3,2,0,1:T(8,128)S(1)} %fusion.18), kind=kOutput, calls=%fused_computation.6 | convolution fusion | flops 1613692928 | bytes 8126464 | tf_op jit(solution)/shard_map/nesh,ehd->nesd/dot_general | solution.py:68
  182.9 4.3 %fusion.1 = bf16[64,1,8,4096]{3,2,0,1:T(8,128)(2,1)} fusion(bf16[64,8,384]{2,1,0:T(8,128)(2,1)S(1)} %fusion.27, bf16[1,4096,384]{2,1,0:T(8,128)(2,1)S(1)} %copy-done.6), kind=kOutput, calls=%fused_computation.7 | convolution fusion | flops 1612709888 | bytes 7733248 | tf_op jit(solution)/shard_map/nesh,edh->nesd/dot_general | solution.py:81
  187.2 7.8 %pad_maximum_fusion = bf16[64,1,16,4096]{3,2,0,1:T(8,128)(2,1)} fusion(bf16[64,1,8,4096]{3,2,0,1:T(8,128)(2,1)} %fusion.1, bf16[64,1,8,4096]{3,2,0,1:T(8,128)(2,1)} %fusion), kind=kLoop, calls=%fused_computation.1 | loop fusion | flops 16777216 | bytes 16777216 | tf_op jit(solution)/shard_map/concatenate | solution.py:82
  195.0 6.2 %fusion.3 = bf16[1,384,4096]{2,1,0:T(8,128)(2,1)} fusion(bf16[64,1,16,4096]{3,2,0,1:T(8,128)(2,1)} %copy-done.1, f32[64,1,8,384]{3,2,0,1:T(8,128)} %copy-done.8), kind=kOutput, calls=%fused_computation.9 | convolution fusion | flops 1613168640 | bytes 8126464 | tf_op jit(solution)/shard_map/nesh,nesd->ehd/dot_general | solution.py:75
  201.3 74.2 %reduce-scatter.2.cloned.1.call-done = bf16[64,1,16,1024]{3,2,0,1:T(8,128)(2,1)} async-done(((bf16[64,1,16,4096]{3,2,0,1:T(8,128)(2,1)}), bf16[64,1,16,1024]{3,2,0,1:T(8,128)(2,1)}) %reduce-scatter.2.cloned.1.call-update) | async-done | bytes 2097168 | tf_op jit(solution)/shard_map/reduce_scatter | solution.py:83
  275.5 10.8 %all-to-all-start.1 = ((bf16[64,1,16,1024]{3,2,1,0:T(8,128)(2,1)}), bf16[64,1,16,1024]{3,2,1,0:T(8,128)(2,1)}, u32[]{:S(2)}, u32[]{:S(2)}) async-start(bf16[64,1,16,1024]{3,2,1,0:T(8,128)(2,1)} %bitcast.125), calls=%async_computation.2 | async-start | bytes 4194304 | tf_op jit(solution)/shard_map/all_to_all | solution.py:84
  286.3 6.3 %fusion.2 = bf16[1,4096,384]{2,1,0:T(8,128)(2,1)} fusion(bf16[64,8,384]{2,1,0:T(8,128)(2,1)} %copy-done.7, bf16[64,1,16,4096]{3,2,0,1:T(8,128)(2,1)} %copy-done.1), kind=kOutput, calls=%fused_computation.8 | convolution fusion | flops 1612185600 | bytes 7733248 | tf_op jit(solution)/shard_map/nesd,nesh->edh/dot_general | solution.py:78
  292.6 44.9 %all-to-all-done.1 = bf16[64,1,16,1024]{3,2,1,0:T(8,128)(2,1)} async-done(((bf16[64,1,16,1024]{3,2,1,0:T(8,128)(2,1)}), bf16[64,1,16,1024]{3,2,1,0:T(8,128)(2,1)}, u32[]{:S(2)}, u32[]{:S(2)}) %all-to-all-start.1) | async-done | bytes 2097184 | tf_op jit(solution)/shard_map/all_to_all | solution.py:84
  337.4 2.5 convolution_convert_fusion.4
  339.9 2.5 convolution_convert_fusion.5
  (29 shorter events, 0.6 us)
Async XLA Ops:
  7.2 169.0 %copy-start = (bf16[1,384,4096]{2,1,0:T(8,128)(2,1)S(1)}, bf16[1,384,4096]{2,1,0:T(8,128)(2,1)}, u32[]{:S(2)}) copy-start(bf16[1,384,4096]{2,1,0:T(8,128)(2,1)} %param.11) | copy-start | bytes 9437188
  7.2 268.3 %reduce-scatter.2.cloned.1.call-start = ((), (), s32[]{:S(2)}) async-start(), calls=%async_computation.3 | async-start | bytes 10485760 | tf_op jit(solution)/shard_map/reduce_scatter | solution.py:83
  9.2 2.2 copy-start.4
  9.2 2.2 copy-start.5
  9.2 2.7 copy-start.2
  9.2 3.2 copy-start.3
  76.8 47.5 %collective-permute-start = (bf16[64,1,16,1024]{3,2,0,1:T(8,128)(2,1)}, bf16[64,1,16,1024]{3,2,0,1:T(8,128)(2,1)}, u32[]{:S(2)}, u32[]{:S(2)}) collective-permute-start(bf16[64,1,16,1024]{3,2,0,1:T(8,128)(2,1)} %bitcast.5), channel_id=1, source_target_pairs={{0,1},{1,2},{2,3},{3,0},{4,5},{5,6},{6,7},{7,4},{8,9},{9,10},{10,1... | collective-permute-start | bytes 6291464 | tf_op jit(solution)/shard_map/ppermute | solution.py:53
  78.4 51.1 %collective-permute-start.1 = (bf16[64,1,16,1024]{3,2,0,1:T(8,128)(2,1)}, bf16[64,1,16,1024]{3,2,0,1:T(8,128)(2,1)}, u32[]{:S(2)}, u32[]{:S(2)}) collective-permute-start(bf16[64,1,16,1024]{3,2,0,1:T(8,128)(2,1)} %bitcast.5), channel_id=1, source_target_pairs={{0,3},{1,0},{2,1},{3,2},{4,7},{5,4},{6,5},{7,6},{8,11},{9,8},{10,9... | collective-permute-start | bytes 6291464 | tf_op jit(solution)/shard_map/ppermute | solution.py:58
  124.4 46.6 %collective-permute-start.2 = (bf16[64,1,16,1024]{3,2,0,1:T(8,128)(2,1)}, bf16[64,1,16,1024]{3,2,0,1:T(8,128)(2,1)}, u32[]{:S(2)}, u32[]{:S(2)}) collective-permute-start(bf16[64,1,16,1024]{3,2,0,1:T(8,128)(2,1)} %collective-permute-done), channel_id=1, source_target_pairs={{0,1},{1,2},{2,3},{3,0},{4,5},{5,6},{6,7},{7,4},{8,9},{9,10},{10,1... | collective-permute-start | bytes 6291464 | tf_op jit(solution)/shard_map/ppermute | solution.py:53
  129.5 43.4 %copy-start.6 = (bf16[1,4096,384]{2,1,0:T(8,128)(2,1)S(1)}, bf16[1,4096,384]{2,1,0:T(8,128)(2,1)}, u32[]{:S(2)}) copy-start(bf16[1,4096,384]{2,1,0:T(8,128)(2,1)} %param.10) | copy-start | bytes 9437188
  172.9 3.2 copy-start.1
  176.1 2.4 copy-start.8
  178.6 4.3 %copy-start.7 = (bf16[64,8,384]{2,1,0:T(8,128)(2,1)}, bf16[64,8,384]{2,1,0:T(8,128)(2,1)S(1)}, u32[]{:S(2)}) copy-start(bf16[64,8,384]{2,1,0:T(8,128)(2,1)S(1)} %fusion.27) | copy-start | bytes 1179652
  275.5 61.9 %all-to-all-start.1 = ((bf16[64,1,16,1024]{3,2,1,0:T(8,128)(2,1)}), bf16[64,1,16,1024]{3,2,1,0:T(8,128)(2,1)}, u32[]{:S(2)}, u32[]{:S(2)}) async-start(bf16[64,1,16,1024]{3,2,1,0:T(8,128)(2,1)} %bitcast.125), calls=%async_computation.2 | async-start | bytes 4194304 | tf_op jit(solution)/shard_map/all_to_all | solution.py:84
Sparse Core Ops, SparseCore 0:
  195.2 80.2 reduce-scatter.1
